TPU v7x, 32 devices: a whole 2x2x4 slice. The times are simulated.
32 devices in a mesh: lon: 8 (over y, x, core), lat: 4 (over z).
Axes of the slice: x: 2, y: 2, z: 4, core: 2. Of those that a mesh axis runs over, the one named last changes fastest.
Arguments:
- latent: bfloat16 [4, 64, 128, 320], P(None, 'lat', 'lon'), may hold values from -28 to 28, as said below
- norm1_gain: float32 [320], replicated, may hold values from 0.1 to 1.9
- norm1_shift: float32 [320], replicated, may hold values from -3 to 3
- conv1_weight: bfloat16 [3, 3, 320, 320], replicated, may hold values from -0.109375 to 0.109375
- conv1_bias: float32 [320], replicated, may hold values from -3 to 3
- emb_shift: float32 [4, 320], replicated, may hold values from -4 to 4
- norm2_gain: float32 [320], replicated, may hold values from 0.1 to 1.9
- norm2_shift: float32 [320], replicated, may hold values from -3 to 3
- conv2_weight: bfloat16 [3, 3, 320, 320], replicated, may hold values from -0.109375 to 0.109375
- conv2_bias: float32 [320], replicated, may hold values from -3 to 3
Outputs:
- block_out: bfloat16 [4, 64, 128, 320], P(None, 'lat', 'lon')
Inputs may be any that keep to these rules, and one draw needn't show every extreme that they name: `latent`: Real-valued activations.
All inputs are finite; a program needn't handle non-finite values.
Results may differ from a plain program's by a relative error of at most 0.007.
Values may be sent and summed in bfloat16 or wider, within the bound.
No kernel may reach another device: no remote copies, remote signals or barrier semaphores. Data moves between devices by JAX's collectives and lax.ppermute only.
A program may use at most 64 MiB of HBM per device.

v0:
```python
import jax
import jax.numpy as jnp
from jax import lax
from jax.sharding import PartitionSpec as P

GROUPS = 32


def padded_2(array, sides, width, wrap):
    for axis, dim in sides:
        devices, length = (lax.axis_size(axis), array.shape[dim])
        up = [(i, (i + 1) % devices) for i in range(devices if wrap else devices - 1)]
        down = [(j, i) for i, j in up]
        last = lax.slice_in_dim(array, length - width, length, axis=dim)
        leading = lax.slice_in_dim(array, 0, width, axis=dim)
        before = lax.ppermute(last, axis, up)
        after = lax.ppermute(leading, axis, down)
        array = jnp.concatenate([before, array, after], axis=dim)
    return array


def from_behind(array, axis, by):
    devices = lax.axis_size(axis)
    return lax.ppermute(array, axis, [(i, (i + by) % devices) for i in range(devices)])


def group_stats(field, cell_count):
    frame_count = field.shape[0]
    grouped = field.reshape(frame_count, -1, GROUPS, field.shape[3] // GROUPS)
    summed, squares = lax.psum(
        (jnp.sum(grouped, axis=(1, 3)), jnp.sum(grouped * grouped, axis=(1, 3))), ("lon", "lat")
    )
    average = summed / cell_count
    variance = squares / cell_count - average * average
    return (average, lax.rsqrt(variance + 1e-05))


def activate(field, average, inverse, norm_gain, norm_shift):
    per_group = field.shape[3] // GROUPS
    per_mean = jnp.repeat(average, per_group, axis=1)[:, None, None, :]
    per_inverse = jnp.repeat(inverse, per_group, axis=1)[:, None, None, :]
    normed = (field - per_mean) * per_inverse * norm_gain + norm_shift
    return jax.nn.silu(normed).astype(jnp.bfloat16)


def sphere_pad(field):
    side_padded = padded_2(field, (("lon", 2),), 1, True)
    both_padded = padded_2(side_padded, (("lat", 1),), 1, False)
    north_row, south_row = from_behind(
        (side_padded[:, 0], side_padded[:, -1]), "lon", lax.axis_size("lon") // 2
    )
    lat_index = lax.axis_index("lat")
    first_row = jnp.where(lat_index == 0, north_row, both_padded[:, 0])
    final_row = jnp.where(lat_index == lax.axis_size("lat") - 1, south_row, both_padded[:, -1])
    return jnp.concatenate([first_row[:, None], both_padded[:, 1:-1], final_row[:, None]], axis=1)


def padded_input(source, cell_count, norm_gain, norm_shift):
    source_f = source.astype(jnp.float32)
    average, inverse = group_stats(source_f, cell_count)
    return sphere_pad(activate(source_f, average, inverse, norm_gain, norm_shift))


def convolve(padded, weight):
    return lax.conv_general_dilated(
        padded,
        weight,
        (1, 1),
        "VALID",
        dimension_numbers=("NHWC", "HWIO", "NHWC"),
        preferred_element_type=jnp.float32,
    )


def on_device(
    latent,
    norm1_gain,
    norm1_shift,
    conv1_weight,
    conv1_bias,
    emb_shift,
    norm2_gain,
    norm2_shift,
    conv2_weight,
    conv2_bias,
):
    per_group = latent.shape[3] // GROUPS
    cell_count = (
        latent.shape[1] * latent.shape[2] * lax.axis_size("lat") * lax.axis_size("lon") * per_group
    )
    first_padded = padded_input(latent, cell_count, norm1_gain, norm1_shift)
    hidden = convolve(first_padded, conv1_weight) + conv1_bias + emb_shift[:, None, None, :]
    hidden = hidden.astype(jnp.bfloat16)
    second_padded = padded_input(hidden, cell_count, norm2_gain, norm2_shift)
    branch = convolve(second_padded, conv2_weight) + conv2_bias
    return (latent.astype(jnp.float32) + branch).astype(jnp.bfloat16)


def solution(mesh):
    placed = (P(None, "lat", "lon", None), P(), P(), P(), P(), P(), P(), P(), P(), P())
    return jax.shard_map(
        on_device,
        mesh=mesh,
        in_specs=placed,
        out_specs=P(None, "lat", "lon", None),
        check_vma=False,
    )
```

profile of v0, /device:TPU:0, one launch (start us, length us, event | category | flops | bytes accessed | tf_op | source)
XLA Modules:
  0.0 154.9 jit_solution(12832509377845679093)
XLA Ops:
  0.0 2.1 %convert_reduce_fusion = (f32[4,320]{1,0:T(4,128)S(1)}, f32[4,320]{1,0:T(4,128)S(1)}) fusion(bf16[4,16,16,320]{3,2,1,0:T(8,128)(2,1)} %param.10), kind=kLoop, calls=%fused_computation.6 | loop fusion | flops 1308160 | bytes 665600 | tf_op jit(solution)/shard_map/reduce_sum | solution.py:31
  2.6 42.0 %all-reduce.1 = (f32[4,32]{1,0:T(4,128)S(1)}, f32[4,32]{1,0:T(4,128)S(1)}) all-reduce(f32[4,32]{1,0:T(4,128)S(1)} %reduce_sum.54, f32[4,32]{1,0:T(4,128)S(1)} %reduce_sum.51), channel_id=1, replica_groups=mesh['lon'=8,'lat'=4] {'lon','lat'}, use_global_device_ids=true, to_apply=%region_5.6 | all-reduce | flops 256 | bytes 2048 | tf_op jit(solution)/shard_map/psum | solution.py:30
  45.0 2.4 %fusion.18 = bf16[4,16,16,320]{3,0,2,1:T(4,128)(2,1)S(1)} fusion(f32[320]{0:T(512)} %param.12, f32[320]{0:T(512)} %param.11, f32[4,320]{1,0:T(4,128)S(1)} %mul.59, f32[4,320]{1,0:T(4,128)S(1)} %sub.26, bf16[4,16,16,320]{3,2,1,0:T(8,128)(2,1)} %param.10), kind=kLoop, calls=%fused_computation.32 | loop fusion | flops 3276800 | bytes 1323520 | tf_op jit(solution)/shard_map/convert_element_type | solution.py:43
  47.5 2.6 %collective-permute-start.1 = (bf16[4,16,1,320]{3,0,2,1:T(4,128)(2,1)S(1)}, bf16[4,16,1,320]{3,0,2,1:T(4,128)(2,1)S(1)}, u32[]{:S(2)}, u32[]{:S(2)}) collective-permute-start(bf16[4,16,1,320]{3,0,2,1:T(4,128)(2,1)S(1)} %get-tuple-element.18), channel_id=1, source_target_pairs={{4,0},{8,4},{12,8},{16,12},{20,16},{24,20},{28,24},{0,28},{5,1},{9... | collective-permute-start | bytes 122888 | tf_op jit(solution)/shard_map/ppermute | solution.py:17
  50.1 1.8 %collective-permute-done = bf16[4,16,1,320]{3,0,2,1:T(4,128)(2,1)S(1)} collective-permute-done((bf16[4,16,1,320]{3,0,2,1:T(4,128)(2,1)S(1)}, bf16[4,16,1,320]{3,0,2,1:T(4,128)(2,1)S(1)}, u32[]{:S(2)}, u32[]{:S(2)}) %collective-permute-start) | collective-permute-done | bytes 40992 | tf_op jit(solution)/shard_map/ppermute | solution.py:16
  52.0 2.3 %collective-permute-start.4 = (bf16[4,18,320]{2,0,1:T(4,128)(2,1)S(1)}, bf16[4,18,320]{2,0,1:T(4,128)(2,1)S(1)}, u32[]{:S(2)}, u32[]{:S(2)}) collective-permute-start(bf16[4,18,320]{2,0,1:T(4,128)(2,1)S(1)} %bitcast.78), channel_id=1, source_target_pairs={{0,16},{4,20},{8,24},{12,28},{16,0},{20,4},{24,8},{28,12},{1,17},{... | collective-permute-start | bytes 138248 | tf_op jit(solution)/shard_map/ppermute | solution.py:24
  54.3 1.3 collective-permute-start.5
  55.6 4.7 %collective-permute-start.3 = (bf16[4,1,18,320]{3,0,2,1:T(4,128)(2,1)S(1)}, bf16[4,1,18,320]{3,0,2,1:T(4,128)(2,1)S(1)}, u32[]{:S(2)}, u32[]{:S(2)}) collective-permute-start(bf16[4,1,18,320]{3,0,2,1:T(4,128)(2,1)S(1)} %get-tuple-element.14), channel_id=1, source_target_pairs={{0,1},{1,2},{2,3},{4,5},{5,6},{6,7},{8,9},{9,10},{10,11},{12,13},{... | collective-permute-start | bytes 138248 | tf_op jit(solution)/shard_map/ppermute | solution.py:16
  60.5 4.1 %collective-permute-done.2 = bf16[4,18,320]{2,0,1:T(4,128)(2,1)S(1)} collective-permute-done((bf16[4,18,320]{2,0,1:T(4,128)(2,1)S(1)}, bf16[4,18,320]{2,0,1:T(4,128)(2,1)S(1)}, u32[]{:S(2)}, u32[]{:S(2)}) %collective-permute-start.2) | collective-permute-done | bytes 46112 | tf_op jit(solution)/shard_map/ppermute | solution.py:24
  64.6 0.9 maximum_bitcast_fusion.1
  66.4 1.0 fusion.5
  68.1 7.1 %fusion.30 = (f32[16,32,3,320]{3,1,2,0:T(8,128)S(1)}, f32[16,32,3,320]{3,1,2,0:T(8,128)}) fusion(f32[16,32,3,320]{3,0,2,1:T(8,128)S(1)} %bitcast.75, f32[320]{0:T(512)S(1)} %copy-done.7, bf16[3,3,320,320]{3,2,1,0:T(8,128)(2,1)S(1)} %copy-done, bf16[18,4,8,5,320]{4,1,3,2,0:T(4,128)(2,1)S(1)} %fusion.5, pred[32,3]{0,1:T(4,128)(4,1)S(1)} %copy-done.9), kind=kOutput, calls=%fused_computation.59 | convolution fusion | flops 2834104320 | bytes 9586016 | tf_op jit(solution)/shard_map/conv_general_dilated | solution.py:65
  75.2 1.4 copy.121
  76.9 3.0 %copy.119 = f32[16,32,3,320]{3,0,2,1:T(8,128)S(1)} copy(f32[16,32,3,320]{3,1,2,0:T(8,128)} %get-tuple-element.24) | data formatting | bytes 3932160 | tf_op jit(solution)/shard_map/convert_element_type | solution.py:59
  80.2 39.4 %all-reduce = (f32[4,32]{1,0:T(4,128)S(1)}, f32[4,32]{1,0:T(4,128)S(1)}) all-reduce(f32[4,32]{1,0:T(4,128)S(1)} %reduce_sum.75, f32[4,32]{1,0:T(4,128)S(1)} %reduce_sum.72), channel_id=1, replica_groups=mesh['lon'=8,'lat'=4] {'lon','lat'}, use_global_device_ids=true, to_apply=%region_11.12 | all-reduce | flops 256 | bytes 2048 | tf_op jit(solution)/shard_map/psum | solution.py:30
  120.4 1.3 copy-done.1
  121.7 1.8 %multiply_convert_fusion = bf16[16,32,3,320]{3,1,2,0:T(8,128)(2,1)S(1)} fusion(f32[16,32,3,320]{3,0,2,1:T(8,128)S(1)} %bitcast.65, f32[16,32,3,320]{3,1,2,0:T(8,128)S(1)} %copy-done.1, f32[16,32,3,320]{3,0,2,1:T(8,128)S(1)} %bitcast.66, f32[320]{0:T(512)S(1)} %copy-done.4, f32[320]{0:T(512)S(1)} %copy-done.5), kind=kLoop, calls=%fused_computation.14 | loop fusion | flops 4423680 | bytes 6883840 | tf_op jit(solution)/shard_map/convert_element_type | solution.py:43
  124.1 2.6 %collective-permute-start.7 = (bf16[4,16,1,320]{3,1,2,0:T(8,128)(2,1)S(1)}, bf16[4,16,1,320]{3,1,2,0:T(8,128)(2,1)S(1)}, u32[]{:S(2)}, u32[]{:S(2)}) collective-permute-start(bf16[4,16,1,320]{3,1,2,0:T(8,128)(2,1)S(1)} %get-tuple-element.16), channel_id=1, source_target_pairs={{4,0},{8,4},{12,8},{16,12},{20,16},{24,20},{28,24},{0,28},{5,1},{9... | collective-permute-start | bytes 122888 | tf_op jit(solution)/shard_map/ppermute | solution.py:17
  126.7 1.8 %collective-permute-done.6 = bf16[4,16,1,320]{3,1,2,0:T(8,128)(2,1)S(1)} collective-permute-done((bf16[4,16,1,320]{3,1,2,0:T(8,128)(2,1)S(1)}, bf16[4,16,1,320]{3,1,2,0:T(8,128)(2,1)S(1)}, u32[]{:S(2)}, u32[]{:S(2)}) %collective-permute-start.6) | collective-permute-done | bytes 40992 | tf_op jit(solution)/shard_map/ppermute | solution.py:16
  128.7 2.3 %collective-permute-start.10 = (bf16[4,18,320]{2,0,1:T(4,128)(2,1)S(1)}, bf16[4,18,320]{2,0,1:T(4,128)(2,1)S(1)}, u32[]{:S(2)}, u32[]{:S(2)}) collective-permute-start(bf16[4,18,320]{2,0,1:T(4,128)(2,1)S(1)} %bitcast.77), channel_id=1, source_target_pairs={{0,16},{4,20},{8,24},{12,28},{16,0},{20,4},{24,8},{28,12},{1,17},{... | collective-permute-start | bytes 138248 | tf_op jit(solution)/shard_map/ppermute | solution.py:24
  131.1 1.3 collective-permute-start.11
  132.4 4.6 %collective-permute-start.9 = (bf16[4,1,18,320]{3,1,2,0:T(2,128)(2,1)S(1)}, bf16[4,1,18,320]{3,1,2,0:T(2,128)(2,1)S(1)}, u32[]{:S(2)}, u32[]{:S(2)}) collective-permute-start(bf16[4,1,18,320]{3,1,2,0:T(2,128)(2,1)S(1)} %get-tuple-element.12), channel_id=1, source_target_pairs={{0,1},{1,2},{2,3},{4,5},{5,6},{6,7},{8,9},{9,10},{10,11},{12,13},{... | collective-permute-start | bytes 138248 | tf_op jit(solution)/shard_map/ppermute | solution.py:16
  137.1 0.6 collective-permute-done.11
  137.9 3.3 %collective-permute-done.8 = bf16[4,18,320]{2,0,1:T(4,128)(2,1)S(1)} collective-permute-done((bf16[4,18,320]{2,0,1:T(4,128)(2,1)S(1)}, bf16[4,18,320]{2,0,1:T(4,128)(2,1)S(1)}, u32[]{:S(2)}, u32[]{:S(2)}) %collective-permute-start.8) | collective-permute-done | bytes 46112 | tf_op jit(solution)/shard_map/ppermute | solution.py:24
  141.3 0.9 maximum_bitcast_fusion
  143.4 1.0 fusion.6
  144.5 0.5 copy-done.6
  145.0 5.0 %select_add_fusion = f32[16,32,3,320]{3,1,2,0:T(8,128)S(1)} fusion(bf16[3,3,320,320]{3,2,1,0:T(8,128)(2,1)S(1)} %copy-done.6, bf16[18,4,8,5,320]{4,1,3,2,0:T(4,128)(2,1)S(1)} %fusion.6, f32[320]{0:T(512)S(1)} %copy-done.8, pred[32,3]{0,1:T(4,128)(4,1)S(1)} %copy-done.9), kind=kOutput, calls=%fused_computation.13 | convolution fusion | flops 2832138240 | bytes 5653856 | tf_op jit(solution)/shard_map/conv_general_dilated | solution.py:65
  150.0 1.4 copy.132
  151.5 1.0 copy-done.2
  152.5 1.4 fusion.17
  154.0 1.0 copy.134
  (71 shorter events, 6.4 us)
Async XLA Ops:
  0.0 67.6 %copy-start = (bf16[3,3,320,320]{3,2,1,0:T(8,128)(2,1)S(1)}, bf16[3,3,320,320]{3,2,1,0:T(8,128)(2,1)}, u32[]{:S(2)}) copy-start(bf16[3,3,320,320]{3,2,1,0:T(8,128)(2,1)} %param.13) | copy-start | bytes 5529604
  47.4 4.5 %collective-permute-start = (bf16[4,16,1,320]{3,0,2,1:T(4,128)(2,1)S(1)}, bf16[4,16,1,320]{3,0,2,1:T(4,128)(2,1)S(1)}, u32[]{:S(2)}, u32[]{:S(2)}) collective-permute-start(bf16[4,16,1,320]{3,0,2,1:T(4,128)(2,1)S(1)} %get-tuple-element.17), channel_id=1, source_target_pairs={{0,4},{4,8},{8,12},{12,16},{16,20},{20,24},{24,28},{28,0},{1,5},{5... | collective-permute-start | bytes 122888 | tf_op jit(solution)/shard_map/ppermute | solution.py:16
  47.5 4.4 %collective-permute-start.1 = (bf16[4,16,1,320]{3,0,2,1:T(4,128)(2,1)S(1)}, bf16[4,16,1,320]{3,0,2,1:T(4,128)(2,1)S(1)}, u32[]{:S(2)}, u32[]{:S(2)}) collective-permute-start(bf16[4,16,1,320]{3,0,2,1:T(4,128)(2,1)S(1)} %get-tuple-element.18), channel_id=1, source_target_pairs={{4,0},{8,4},{12,8},{16,12},{20,16},{24,20},{28,24},{0,28},{5,1},{9... | collective-permute-start | bytes 122888 | tf_op jit(solution)/shard_map/ppermute | solution.py:17
  52.0 8.5 %collective-permute-start.4 = (bf16[4,18,320]{2,0,1:T(4,128)(2,1)S(1)}, bf16[4,18,320]{2,0,1:T(4,128)(2,1)S(1)}, u32[]{:S(2)}, u32[]{:S(2)}) collective-permute-start(bf16[4,18,320]{2,0,1:T(4,128)(2,1)S(1)} %bitcast.78), channel_id=1, source_target_pairs={{0,16},{4,20},{8,24},{12,28},{16,0},{20,4},{24,8},{28,12},{1,17},{... | collective-permute-start | bytes 138248 | tf_op jit(solution)/shard_map/ppermute | solution.py:24
  54.3 6.1 %collective-permute-start.5 = (bf16[4,1,18,320]{3,0,2,1:T(4,128)(2,1)S(1)}, bf16[4,1,18,320]{3,0,2,1:T(4,128)(2,1)S(1)}, u32[]{:S(2)}, u32[]{:S(2)}) collective-permute-start(bf16[4,1,18,320]{3,0,2,1:T(4,128)(2,1)S(1)} %get-tuple-element.13), channel_id=1, source_target_pairs={{1,0},{2,1},{3,2},{5,4},{6,5},{7,6},{9,8},{10,9},{11,10},{13,12},{... | collective-permute-start | bytes 138248 | tf_op jit(solution)/shard_map/ppermute | solution.py:17
  55.6 9.0 %collective-permute-start.3 = (bf16[4,1,18,320]{3,0,2,1:T(4,128)(2,1)S(1)}, bf16[4,1,18,320]{3,0,2,1:T(4,128)(2,1)S(1)}, u32[]{:S(2)}, u32[]{:S(2)}) collective-permute-start(bf16[4,1,18,320]{3,0,2,1:T(4,128)(2,1)S(1)} %get-tuple-element.14), channel_id=1, source_target_pairs={{0,1},{1,2},{2,3},{4,5},{5,6},{6,7},{8,9},{9,10},{10,11},{12,13},{... | collective-permute-start | bytes 138248 | tf_op jit(solution)/shard_map/ppermute | solution.py:16
  60.4 4.2 %collective-permute-start.2 = (bf16[4,18,320]{2,0,1:T(4,128)(2,1)S(1)}, bf16[4,18,320]{2,0,1:T(4,128)(2,1)S(1)}, u32[]{:S(2)}, u32[]{:S(2)}) collective-permute-start(bf16[4,18,320]{2,0,1:T(4,128)(2,1)S(1)} %bitcast.79), channel_id=1, source_target_pairs={{0,16},{4,20},{8,24},{12,28},{16,0},{20,4},{24,8},{28,12},{1,17},{... | collective-permute-start | bytes 138248 | tf_op jit(solution)/shard_map/ppermute | solution.py:24
  66.4 1.1 copy-start.3
  67.4 0.7 copy-start.7
  67.4 0.7 copy-start.9
  120.1 1.7 %copy-start.1 = (f32[16,32,3,320]{3,1,2,0:T(8,128)S(1)}, f32[16,32,3,320]{3,1,2,0:T(8,128)}, u32[]{:S(2)}) copy-start(f32[16,32,3,320]{3,1,2,0:T(8,128)} %get-tuple-element.24) | copy-start | bytes 5898244
  120.1 1.7 %copy-start.4 = (f32[320]{0:T(512)S(1)}, f32[320]{0:T(512)}, u32[]{:S(2)}) copy-start(f32[320]{0:T(512)} %param.17) | copy-start | bytes 3844
  120.1 1.7 %copy-start.5 = (f32[320]{0:T(512)S(1)}, f32[320]{0:T(512)}, u32[]{:S(2)}) copy-start(f32[320]{0:T(512)} %param.16) | copy-start | bytes 3844
  124.0 4.5 %collective-permute-start.6 = (bf16[4,16,1,320]{3,1,2,0:T(8,128)(2,1)S(1)}, bf16[4,16,1,320]{3,1,2,0:T(8,128)(2,1)S(1)}, u32[]{:S(2)}, u32[]{:S(2)}) collective-permute-start(bf16[4,16,1,320]{3,1,2,0:T(8,128)(2,1)S(1)} %get-tuple-element.15), channel_id=1, source_target_pairs={{0,4},{4,8},{8,12},{12,16},{16,20},{20,24},{24,28},{28,0},{1,5},{5... | collective-permute-start | bytes 122888 | tf_op jit(solution)/shard_map/ppermute | solution.py:16
  124.1 4.4 %collective-permute-start.7 = (bf16[4,16,1,320]{3,1,2,0:T(8,128)(2,1)S(1)}, bf16[4,16,1,320]{3,1,2,0:T(8,128)(2,1)S(1)}, u32[]{:S(2)}, u32[]{:S(2)}) collective-permute-start(bf16[4,16,1,320]{3,1,2,0:T(8,128)(2,1)S(1)} %get-tuple-element.16), channel_id=1, source_target_pairs={{4,0},{8,4},{12,8},{16,12},{20,16},{24,20},{28,24},{0,28},{5,1},{9... | collective-permute-start | bytes 122888 | tf_op jit(solution)/shard_map/ppermute | solution.py:17
  128.7 8.3 %collective-permute-start.10 = (bf16[4,18,320]{2,0,1:T(4,128)(2,1)S(1)}, bf16[4,18,320]{2,0,1:T(4,128)(2,1)S(1)}, u32[]{:S(2)}, u32[]{:S(2)}) collective-permute-start(bf16[4,18,320]{2,0,1:T(4,128)(2,1)S(1)} %bitcast.77), channel_id=1, source_target_pairs={{0,16},{4,20},{8,24},{12,28},{16,0},{20,4},{24,8},{28,12},{1,17},{... | collective-permute-start | bytes 138248 | tf_op jit(solution)/shard_map/ppermute | solution.py:24
  131.1 6.6 %collective-permute-start.11 = (bf16[4,1,18,320]{3,1,2,0:T(2,128)(2,1)S(1)}, bf16[4,1,18,320]{3,1,2,0:T(2,128)(2,1)S(1)}, u32[]{:S(2)}, u32[]{:S(2)}) collective-permute-start(bf16[4,1,18,320]{3,1,2,0:T(2,128)(2,1)S(1)} %get-tuple-element.11), channel_id=1, source_target_pairs={{1,0},{2,1},{3,2},{5,4},{6,5},{7,6},{9,8},{10,9},{11,10},{13,12},{... | collective-permute-start | bytes 138248 | tf_op jit(solution)/shard_map/ppermute | solution.py:17
  132.4 8.8 %collective-permute-start.9 = (bf16[4,1,18,320]{3,1,2,0:T(2,128)(2,1)S(1)}, bf16[4,1,18,320]{3,1,2,0:T(2,128)(2,1)S(1)}, u32[]{:S(2)}, u32[]{:S(2)}) collective-permute-start(bf16[4,1,18,320]{3,1,2,0:T(2,128)(2,1)S(1)} %get-tuple-element.12), channel_id=1, source_target_pairs={{0,1},{1,2},{2,3},{4,5},{5,6},{6,7},{8,9},{9,10},{10,11},{12,13},{... | collective-permute-start | bytes 138248 | tf_op jit(solution)/shard_map/ppermute | solution.py:16
  137.0 4.2 %collective-permute-start.8 = (bf16[4,18,320]{2,0,1:T(4,128)(2,1)S(1)}, bf16[4,18,320]{2,0,1:T(4,128)(2,1)S(1)}, u32[]{:S(2)}, u32[]{:S(2)}) collective-permute-start(bf16[4,18,320]{2,0,1:T(4,128)(2,1)S(1)} %bitcast.76), channel_id=1, source_target_pairs={{0,16},{4,20},{8,24},{12,28},{16,0},{20,4},{24,8},{28,12},{1,17},{... | collective-permute-start | bytes 138248 | tf_op jit(solution)/shard_map/ppermute | solution.py:24
  143.4 1.6 %copy-start.6 = (bf16[3,3,320,320]{3,2,1,0:T(8,128)(2,1)S(1)}, bf16[3,3,320,320]{3,2,1,0:T(8,128)(2,1)}, u32[]{:S(2)}) copy-start(bf16[3,3,320,320]{3,2,1,0:T(8,128)(2,1)} %param.18) | copy-start | bytes 5529604
  143.4 1.6 %copy-start.8 = (f32[320]{0:T(512)S(1)}, f32[320]{0:T(512)}, u32[]{:S(2)}) copy-start(f32[320]{0:T(512)} %param.19) | copy-start | bytes 3844
  151.4 1.1 copy-start.2
where the time goes:
time: 156 us; the launch traced here: 155 us
  blocking collectives  81.4 us (52%)
  starting transfers between devices  22.1 us (14%)
  local copies, waits for them, and re-layouts  14.6 us (9%)
  other arithmetic  12.7 us (8%)
  matrix products  12.1 us (8%)
  waiting for transfers between devices  11.6 us (7%)
    psum x2, blocking collectives, group_stats(): lax.psum((jnp.sum(grouped, axis=(1, 3)), jnp.sum(grouped * grouped, axis=...  81.4 us
    conv_general_dilated x2, matrix products, convolve(): lax.conv_general_dilated(padded, weight, (1, 1), 'VALID', dimension_numbe...  12.1 us
    ppermute x4, starting transfers between devices, padded_2(): before = lax.ppermute(last, axis, up)  9.4 us
    ppermute x4, starting transfers between devices, padded_2(): after = lax.ppermute(leading, axis, down)  7.82 us
    ppermute x4, waiting for transfers between devices, from_behind(): lax.ppermute(array, axis, [(i, (i + by) % devices) for i in range(devices)])  7.42 us
    ppermute x4, starting transfers between devices, from_behind(): lax.ppermute(array, axis, [(i, (i + by) % devices) for i in range(devices)])  4.85 us
    convert_element_type x2, other arithmetic, activate(): return jax.nn.silu(normed).astype(jnp.bfloat16)  4.24 us
    unnamed x21, local copies, waits for them, and re-layouts  3.76 us
  transfers between devices with their start and end apart: 12, of which 5 were waited for; matrix products, arithmetic and copies ran while one was open for 0% of the time, Pallas kernels for 0%

commit v1 on v0

--- a/solution.py
+++ b/solution.py
@@ -28,7 +28,8 @@
     frame_count = field.shape[0]
     grouped = field.reshape(frame_count, -1, GROUPS, field.shape[3] // GROUPS)
     summed, squares = lax.psum(
-        (jnp.sum(grouped, axis=(1, 3)), jnp.sum(grouped * grouped, axis=(1, 3))), ("lon", "lat")
+        lax.psum((jnp.sum(grouped, axis=(1, 3)), jnp.sum(grouped * grouped, axis=(1, 3))), "lon"),
+        "lat",
     )
     average = summed / cell_count
     variance = squares / cell_count - average * average

time: 156 us -> 120 us (0.77)
  blocking collectives: 81.4 us -> 48.4 us
  waiting for transfers between devices: 11.6 us -> 9.65 us
    psum x2, blocking collectives: 81.4 us -> 27.6 us  [group_stats(): lax.psum((jnp.sum(grouped, axis=(1, 3)), jnp.sum(grouped * grouped, axis=...]
    psum x0 -> x2, blocking collectives: none -> 20.8 us  [group_stats(): lax.psum(lax.psum((jnp.sum(grouped, axis=(1, 3)), jnp.sum(grouped * group...]
where the time goes in v1:
time: 120 us; the launch traced here: 119 us
  blocking collectives  48.4 us (40%)
  starting transfers between devices  21.5 us (18%)
  local copies, waits for them, and re-layouts  14.6 us (12%)
  other arithmetic  12.7 us (11%)
  matrix products  12.1 us (10%)
  waiting for transfers between devices  9.65 us (8%)
    psum x2, blocking collectives, group_stats(): lax.psum((jnp.sum(grouped, axis=(1, 3)), jnp.sum(grouped * grouped, axis=...  27.6 us
    psum x2, blocking collectives, group_stats(): lax.psum(lax.psum((jnp.sum(grouped, axis=(1, 3)), jnp.sum(grouped * group...  20.8 us
    conv_general_dilated x2, matrix products, convolve(): lax.conv_general_dilated(padded, weight, (1, 1), 'VALID', dimension_numbe...  12.1 us
    ppermute x4, starting transfers between devices, padded_2(): before = lax.ppermute(last, axis, up)  9.4 us
    ppermute x4, starting transfers between devices, padded_2(): after = lax.ppermute(leading, axis, down)  7.82 us
    ppermute x4, waiting for transfers between devices, from_behind(): lax.ppermute(array, axis, [(i, (i + by) % devices) for i in range(devices)])  5.93 us
    ppermute x4, starting transfers between devices, from_behind(): lax.ppermute(array, axis, [(i, (i + by) % devices) for i in range(devices)])  4.31 us
    convert_element_type x2, other arithmetic, activate(): return jax.nn.silu(normed).astype(jnp.bfloat16)  4.24 us
  transfers between devices with their start and end apart: 12, of which 5 were waited for; matrix products, arithmetic and copies ran while one was open for 0% of the time, Pallas kernels for 0%

profile of v1, /device:TPU:0, one launch (start us, length us, event | category | flops | bytes accessed | tf_op | source)
XLA Modules:
  0.0 119.4 jit_solution(3777234880564308092)
XLA Ops:
  0.0 2.1 %convert_reduce_fusion = (f32[4,320]{1,0:T(4,128)S(1)}, f32[4,320]{1,0:T(4,128)S(1)}) fusion(bf16[4,16,16,320]{3,2,1,0:T(8,128)(2,1)} %param.10), kind=kLoop, calls=%fused_computation.6 | loop fusion | flops 1308160 | bytes 665600 | tf_op jit(solution)/shard_map/reduce_sum | solution.py:31
  2.6 15.2 %all-reduce.1 = (f32[4,32]{1,0:T(4,128)S(1)}, f32[4,32]{1,0:T(4,128)S(1)}) all-reduce(f32[4,32]{1,0:T(4,128)S(1)} %reduce_sum.54, f32[4,32]{1,0:T(4,128)S(1)} %reduce_sum.51), channel_id=1, replica_groups=mesh['lon'=8,'lat'=4] {'lon'}, use_global_device_ids=true, to_apply=%region_6.7 | all-reduce | flops 256 | bytes 2048 | tf_op jit(solution)/shard_map/psum | solution.py:31
  17.7 11.9 %all-reduce.3 = (f32[4,32]{1,0:T(4,128)S(1)}, f32[4,32]{1,0:T(4,128)S(1)}) all-reduce(f32[4,32]{1,0:T(4,128)S(1)} %get-tuple-element.9, f32[4,32]{1,0:T(4,128)S(1)} %get-tuple-element.10), channel_id=1, replica_groups=mesh['lon'=8,'lat'=4] {'lat'}, use_global_device_ids=true, to_apply=%region_7.8 | all-reduce | flops 256 | bytes 2048 | tf_op jit(solution)/shard_map/psum | solution.py:30
  30.1 2.4 %fusion.18 = bf16[4,16,16,320]{3,0,2,1:T(4,128)(2,1)S(1)} fusion(f32[320]{0:T(512)} %param.12, f32[320]{0:T(512)} %param.11, f32[4,320]{1,0:T(4,128)S(1)} %mul.59, f32[4,320]{1,0:T(4,128)S(1)} %sub.26, bf16[4,16,16,320]{3,2,1,0:T(8,128)(2,1)} %param.10), kind=kLoop, calls=%fused_computation.32 | loop fusion | flops 3276800 | bytes 1323520 | tf_op jit(solution)/shard_map/convert_element_type | solution.py:44
  32.6 2.6 %collective-permute-start.1 = (bf16[4,16,1,320]{3,0,2,1:T(4,128)(2,1)S(1)}, bf16[4,16,1,320]{3,0,2,1:T(4,128)(2,1)S(1)}, u32[]{:S(2)}, u32[]{:S(2)}) collective-permute-start(bf16[4,16,1,320]{3,0,2,1:T(4,128)(2,1)S(1)} %get-tuple-element.22), channel_id=1, source_target_pairs={{4,0},{8,4},{12,8},{16,12},{20,16},{24,20},{28,24},{0,28},{5,1},{9... | collective-permute-start | bytes 122888 | tf_op jit(solution)/shard_map/ppermute | solution.py:17
  35.3 1.8 %collective-permute-done = bf16[4,16,1,320]{3,0,2,1:T(4,128)(2,1)S(1)} collective-permute-done((bf16[4,16,1,320]{3,0,2,1:T(4,128)(2,1)S(1)}, bf16[4,16,1,320]{3,0,2,1:T(4,128)(2,1)S(1)}, u32[]{:S(2)}, u32[]{:S(2)}) %collective-permute-start) | collective-permute-done | bytes 40992 | tf_op jit(solution)/shard_map/ppermute | solution.py:16
  37.7 1.3 %collective-permute-start.5 = (bf16[4,1,18,320]{3,0,2,1:T(4,128)(2,1)S(1)}, bf16[4,1,18,320]{3,0,2,1:T(4,128)(2,1)S(1)}, u32[]{:S(2)}, u32[]{:S(2)}) collective-permute-start(bf16[4,1,18,320]{3,0,2,1:T(4,128)(2,1)S(1)} %get-tuple-element.17), channel_id=1, source_target_pairs={{1,0},{2,1},{3,2},{5,4},{6,5},{7,6},{9,8},{10,9},{11,10},{13,12},{... | collective-permute-start | bytes 138248 | tf_op jit(solution)/shard_map/ppermute | solution.py:17
  39.0 4.7 %collective-permute-start.3 = (bf16[4,1,18,320]{3,0,2,1:T(4,128)(2,1)S(1)}, bf16[4,1,18,320]{3,0,2,1:T(4,128)(2,1)S(1)}, u32[]{:S(2)}, u32[]{:S(2)}) collective-permute-start(bf16[4,1,18,320]{3,0,2,1:T(4,128)(2,1)S(1)} %get-tuple-element.18), channel_id=1, source_target_pairs={{0,1},{1,2},{2,3},{4,5},{5,6},{6,7},{8,9},{9,10},{10,11},{12,13},{... | collective-permute-start | bytes 138248 | tf_op jit(solution)/shard_map/ppermute | solution.py:16
  43.7 1.6 %collective-permute-start.2 = (bf16[4,18,320]{2,0,1:T(4,128)(2,1)S(1)}, bf16[4,18,320]{2,0,1:T(4,128)(2,1)S(1)}, u32[]{:S(2)}, u32[]{:S(2)}) collective-permute-start(bf16[4,18,320]{2,0,1:T(4,128)(2,1)S(1)} %bitcast.79), channel_id=1, source_target_pairs={{0,16},{4,20},{8,24},{12,28},{16,0},{20,4},{24,8},{28,12},{1,17},{... | collective-permute-start | bytes 138248 | tf_op jit(solution)/shard_map/ppermute | solution.py:24
  45.4 2.6 %collective-permute-done.2 = bf16[4,18,320]{2,0,1:T(4,128)(2,1)S(1)} collective-permute-done((bf16[4,18,320]{2,0,1:T(4,128)(2,1)S(1)}, bf16[4,18,320]{2,0,1:T(4,128)(2,1)S(1)}, u32[]{:S(2)}, u32[]{:S(2)}) %collective-permute-start.2) | collective-permute-done | bytes 46112 | tf_op jit(solution)/shard_map/ppermute | solution.py:24
  48.0 0.9 maximum_bitcast_fusion.1
  49.7 1.0 fusion.5
  51.5 7.1 %fusion.30 = (f32[16,32,3,320]{3,1,2,0:T(8,128)S(1)}, f32[16,32,3,320]{3,1,2,0:T(8,128)}) fusion(f32[16,32,3,320]{3,0,2,1:T(8,128)S(1)} %bitcast.75, f32[320]{0:T(512)S(1)} %copy-done.7, bf16[3,3,320,320]{3,2,1,0:T(8,128)(2,1)S(1)} %copy-done, bf16[18,4,8,5,320]{4,1,3,2,0:T(4,128)(2,1)S(1)} %fusion.5, pred[32,3]{0,1:T(4,128)(4,1)S(1)} %copy-done.9), kind=kOutput, calls=%fused_computation.59 | convolution fusion | flops 2834104320 | bytes 9586016 | tf_op jit(solution)/shard_map/conv_general_dilated | solution.py:66
  58.5 1.4 %copy.121 = f32[16,32,3,320]{3,0,2,1:T(8,128)S(1)} copy(f32[16,32,3,320]{3,1,2,0:T(8,128)S(1)} %get-tuple-element.27) | data formatting | bytes 3932160 | tf_op jit(solution)/shard_map/mul | solution.py:31
  60.2 3.0 %copy.119 = f32[16,32,3,320]{3,0,2,1:T(8,128)S(1)} copy(f32[16,32,3,320]{3,1,2,0:T(8,128)} %get-tuple-element.28) | data formatting | bytes 3932160 | tf_op jit(solution)/shard_map/convert_element_type | solution.py:60
  63.6 12.5 %all-reduce = (f32[4,32]{1,0:T(4,128)S(1)}, f32[4,32]{1,0:T(4,128)S(1)}) all-reduce(f32[4,32]{1,0:T(4,128)S(1)} %reduce_sum.75, f32[4,32]{1,0:T(4,128)S(1)} %reduce_sum.72), channel_id=1, replica_groups=mesh['lon'=8,'lat'=4] {'lon'}, use_global_device_ids=true, to_apply=%region_14.15 | all-reduce | flops 256 | bytes 2048 | tf_op jit(solution)/shard_map/psum | solution.py:31
  76.0 8.9 %all-reduce.2 = (f32[4,32]{1,0:T(4,128)S(1)}, f32[4,32]{1,0:T(4,128)S(1)}) all-reduce(f32[4,32]{1,0:T(4,128)S(1)} %get-tuple-element.7, f32[4,32]{1,0:T(4,128)S(1)} %get-tuple-element.8), channel_id=1, replica_groups=mesh['lon'=8,'lat'=4] {'lat'}, use_global_device_ids=true, to_apply=%region_15.16 | all-reduce | flops 256 | bytes 2048 | tf_op jit(solution)/shard_map/psum | solution.py:30
  85.7 1.3 %copy-done.1 = f32[16,32,3,320]{3,1,2,0:T(8,128)S(1)} copy-done((f32[16,32,3,320]{3,1,2,0:T(8,128)S(1)}, f32[16,32,3,320]{3,1,2,0:T(8,128)}, u32[]{:S(2)}) %copy-start.1) | copy-done | bytes 1966104
  87.0 1.8 %multiply_convert_fusion = bf16[16,32,3,320]{3,1,2,0:T(8,128)(2,1)S(1)} fusion(f32[16,32,3,320]{3,0,2,1:T(8,128)S(1)} %bitcast.65, f32[16,32,3,320]{3,1,2,0:T(8,128)S(1)} %copy-done.1, f32[16,32,3,320]{3,0,2,1:T(8,128)S(1)} %bitcast.66, f32[320]{0:T(512)S(1)} %copy-done.4, f32[320]{0:T(512)S(1)} %copy-done.5), kind=kLoop, calls=%fused_computation.14 | loop fusion | flops 4423680 | bytes 6883840 | tf_op jit(solution)/shard_map/convert_element_type | solution.py:44
  89.4 2.6 %collective-permute-start.7 = (bf16[4,16,1,320]{3,1,2,0:T(8,128)(2,1)S(1)}, bf16[4,16,1,320]{3,1,2,0:T(8,128)(2,1)S(1)}, u32[]{:S(2)}, u32[]{:S(2)}) collective-permute-start(bf16[4,16,1,320]{3,1,2,0:T(8,128)(2,1)S(1)} %get-tuple-element.20), channel_id=1, source_target_pairs={{4,0},{8,4},{12,8},{16,12},{20,16},{24,20},{28,24},{0,28},{5,1},{9... | collective-permute-start | bytes 122888 | tf_op jit(solution)/shard_map/ppermute | solution.py:17
  92.0 1.8 %collective-permute-done.6 = bf16[4,16,1,320]{3,1,2,0:T(8,128)(2,1)S(1)} collective-permute-done((bf16[4,16,1,320]{3,1,2,0:T(8,128)(2,1)S(1)}, bf16[4,16,1,320]{3,1,2,0:T(8,128)(2,1)S(1)}, u32[]{:S(2)}, u32[]{:S(2)}) %collective-permute-start.6) | collective-permute-done | bytes 40992 | tf_op jit(solution)/shard_map/ppermute | solution.py:16
  94.0 1.6 %collective-permute-start.10 = (bf16[4,18,320]{2,0,1:T(4,128)(2,1)S(1)}, bf16[4,18,320]{2,0,1:T(4,128)(2,1)S(1)}, u32[]{:S(2)}, u32[]{:S(2)}) collective-permute-start(bf16[4,18,320]{2,0,1:T(4,128)(2,1)S(1)} %bitcast.77), channel_id=1, source_target_pairs={{0,16},{4,20},{8,24},{12,28},{16,0},{20,4},{24,8},{28,12},{1,17},{... | collective-permute-start | bytes 138248 | tf_op jit(solution)/shard_map/ppermute | solution.py:24
  95.6 1.3 %collective-permute-start.11 = (bf16[4,1,18,320]{3,1,2,0:T(2,128)(2,1)S(1)}, bf16[4,1,18,320]{3,1,2,0:T(2,128)(2,1)S(1)}, u32[]{:S(2)}, u32[]{:S(2)}) collective-permute-start(bf16[4,1,18,320]{3,1,2,0:T(2,128)(2,1)S(1)} %get-tuple-element.15), channel_id=1, source_target_pairs={{1,0},{2,1},{3,2},{5,4},{6,5},{7,6},{9,8},{10,9},{11,10},{13,12},{... | collective-permute-start | bytes 138248 | tf_op jit(solution)/shard_map/ppermute | solution.py:17
  96.9 4.6 %collective-permute-start.9 = (bf16[4,1,18,320]{3,1,2,0:T(2,128)(2,1)S(1)}, bf16[4,1,18,320]{3,1,2,0:T(2,128)(2,1)S(1)}, u32[]{:S(2)}, u32[]{:S(2)}) collective-permute-start(bf16[4,1,18,320]{3,1,2,0:T(2,128)(2,1)S(1)} %get-tuple-element.16), channel_id=1, source_target_pairs={{0,1},{1,2},{2,3},{4,5},{5,6},{6,7},{8,9},{9,10},{10,11},{12,13},{... | collective-permute-start | bytes 138248 | tf_op jit(solution)/shard_map/ppermute | solution.py:16
  102.4 3.3 %collective-permute-done.8 = bf16[4,18,320]{2,0,1:T(4,128)(2,1)S(1)} collective-permute-done((bf16[4,18,320]{2,0,1:T(4,128)(2,1)S(1)}, bf16[4,18,320]{2,0,1:T(4,128)(2,1)S(1)}, u32[]{:S(2)}, u32[]{:S(2)}) %collective-permute-start.8) | collective-permute-done | bytes 46112 | tf_op jit(solution)/shard_map/ppermute | solution.py:24
  105.8 0.9 maximum_bitcast_fusion
  107.9 1.0 fusion.6
  109.5 5.0 %select_add_fusion = f32[16,32,3,320]{3,1,2,0:T(8,128)S(1)} fusion(bf16[3,3,320,320]{3,2,1,0:T(8,128)(2,1)S(1)} %copy-done.6, bf16[18,4,8,5,320]{4,1,3,2,0:T(4,128)(2,1)S(1)} %fusion.6, f32[320]{0:T(512)S(1)} %copy-done.8, pred[32,3]{0,1:T(4,128)(4,1)S(1)} %copy-done.9), kind=kOutput, calls=%fused_computation.13 | convolution fusion | flops 2832138240 | bytes 5653856 | tf_op jit(solution)/shard_map/conv_general_dilated | solution.py:66
  114.5 1.4 %copy.132 = f32[16,32,3,320]{3,0,2,1:T(8,128)S(1)} copy(f32[16,32,3,320]{3,1,2,0:T(8,128)S(1)} %select_add_fusion) | data formatting | bytes 3932160 | tf_op jit(solution)/shard_map/add | solution.py:96
  116.0 1.0 copy-done.2
  117.0 1.4 %fusion.17 = bf16[4,16,16,320]{3,0,2,1:T(4,128)(2,1)S(1)} fusion(f32[16,4,16,320]{3,0,2,1:T(8,128)S(1)} %slice.51, bf16[4,16,16,320]{3,2,1,0:T(8,128)(2,1)S(1)} %copy-done.2), kind=kLoop, calls=%fused_computation.28 | loop fusion | flops 983040 | bytes 2621440 | tf_op jit(solution)/shard_map/convert_element_type | solution.py:97
  118.5 1.0 copy.134
  (73 shorter events, 8.1 us)
Async XLA Ops:
  0.0 51.0 %copy-start = (bf16[3,3,320,320]{3,2,1,0:T(8,128)(2,1)S(1)}, bf16[3,3,320,320]{3,2,1,0:T(8,128)(2,1)}, u32[]{:S(2)}) copy-start(bf16[3,3,320,320]{3,2,1,0:T(8,128)(2,1)} %param.13) | copy-start | bytes 5529604
  32.6 4.5 %collective-permute-start = (bf16[4,16,1,320]{3,0,2,1:T(4,128)(2,1)S(1)}, bf16[4,16,1,320]{3,0,2,1:T(4,128)(2,1)S(1)}, u32[]{:S(2)}, u32[]{:S(2)}) collective-permute-start(bf16[4,16,1,320]{3,0,2,1:T(4,128)(2,1)S(1)} %get-tuple-element.21), channel_id=1, source_target_pairs={{0,4},{4,8},{8,12},{12,16},{16,20},{20,24},{24,28},{28,0},{1,5},{5... | collective-permute-start | bytes 122888 | tf_op jit(solution)/shard_map/ppermute | solution.py:16
  32.6 4.4 %collective-permute-start.1 = (bf16[4,16,1,320]{3,0,2,1:T(4,128)(2,1)S(1)}, bf16[4,16,1,320]{3,0,2,1:T(4,128)(2,1)S(1)}, u32[]{:S(2)}, u32[]{:S(2)}) collective-permute-start(bf16[4,16,1,320]{3,0,2,1:T(4,128)(2,1)S(1)} %get-tuple-element.22), channel_id=1, source_target_pairs={{4,0},{8,4},{12,8},{16,12},{20,16},{24,20},{28,24},{0,28},{5,1},{9... | collective-permute-start | bytes 122888 | tf_op jit(solution)/shard_map/ppermute | solution.py:17
  37.1 8.2 %collective-permute-start.4 = (bf16[4,18,320]{2,0,1:T(4,128)(2,1)S(1)}, bf16[4,18,320]{2,0,1:T(4,128)(2,1)S(1)}, u32[]{:S(2)}, u32[]{:S(2)}) collective-permute-start(bf16[4,18,320]{2,0,1:T(4,128)(2,1)S(1)} %bitcast.78), channel_id=1, source_target_pairs={{0,16},{4,20},{8,24},{12,28},{16,0},{20,4},{24,8},{28,12},{1,17},{... | collective-permute-start | bytes 138248 | tf_op jit(solution)/shard_map/ppermute | solution.py:24
  37.7 7.6 %collective-permute-start.5 = (bf16[4,1,18,320]{3,0,2,1:T(4,128)(2,1)S(1)}, bf16[4,1,18,320]{3,0,2,1:T(4,128)(2,1)S(1)}, u32[]{:S(2)}, u32[]{:S(2)}) collective-permute-start(bf16[4,1,18,320]{3,0,2,1:T(4,128)(2,1)S(1)} %get-tuple-element.17), channel_id=1, source_target_pairs={{1,0},{2,1},{3,2},{5,4},{6,5},{7,6},{9,8},{10,9},{11,10},{13,12},{... | collective-permute-start | bytes 138248 | tf_op jit(solution)/shard_map/ppermute | solution.py:17
  39.0 9.0 %collective-permute-start.3 = (bf16[4,1,18,320]{3,0,2,1:T(4,128)(2,1)S(1)}, bf16[4,1,18,320]{3,0,2,1:T(4,128)(2,1)S(1)}, u32[]{:S(2)}, u32[]{:S(2)}) collective-permute-start(bf16[4,1,18,320]{3,0,2,1:T(4,128)(2,1)S(1)} %get-tuple-element.18), channel_id=1, source_target_pairs={{0,1},{1,2},{2,3},{4,5},{5,6},{6,7},{8,9},{9,10},{10,11},{12,13},{... | collective-permute-start | bytes 138248 | tf_op jit(solution)/shard_map/ppermute | solution.py:16
  43.7 4.2 %collective-permute-start.2 = (bf16[4,18,320]{2,0,1:T(4,128)(2,1)S(1)}, bf16[4,18,320]{2,0,1:T(4,128)(2,1)S(1)}, u32[]{:S(2)}, u32[]{:S(2)}) collective-permute-start(bf16[4,18,320]{2,0,1:T(4,128)(2,1)S(1)} %bitcast.79), channel_id=1, source_target_pairs={{0,16},{4,20},{8,24},{12,28},{16,0},{20,4},{24,8},{28,12},{1,17},{... | collective-permute-start | bytes 138248 | tf_op jit(solution)/shard_map/ppermute | solution.py:24
  49.7 1.1 copy-start.3
  50.8 0.7 copy-start.7
  50.8 0.7 copy-start.9
  85.3 1.7 %copy-start.1 = (f32[16,32,3,320]{3,1,2,0:T(8,128)S(1)}, f32[16,32,3,320]{3,1,2,0:T(8,128)}, u32[]{:S(2)}) copy-start(f32[16,32,3,320]{3,1,2,0:T(8,128)} %get-tuple-element.28) | copy-start | bytes 5898244
  85.3 1.7 %copy-start.4 = (f32[320]{0:T(512)S(1)}, f32[320]{0:T(512)}, u32[]{:S(2)}) copy-start(f32[320]{0:T(512)} %param.17) | copy-start | bytes 3844
  85.3 1.7 %copy-start.5 = (f32[320]{0:T(512)S(1)}, f32[320]{0:T(512)}, u32[]{:S(2)}) copy-start(f32[320]{0:T(512)} %param.16) | copy-start | bytes 3844
  89.3 4.5 %collective-permute-start.6 = (bf16[4,16,1,320]{3,1,2,0:T(8,128)(2,1)S(1)}, bf16[4,16,1,320]{3,1,2,0:T(8,128)(2,1)S(1)}, u32[]{:S(2)}, u32[]{:S(2)}) collective-permute-start(bf16[4,16,1,320]{3,1,2,0:T(8,128)(2,1)S(1)} %get-tuple-element.19), channel_id=1, source_target_pairs={{0,4},{4,8},{8,12},{12,16},{16,20},{20,24},{24,28},{28,0},{1,5},{5... | collective-permute-start | bytes 122888 | tf_op jit(solution)/shard_map/ppermute | solution.py:16
  89.4 4.4 %collective-permute-start.7 = (bf16[4,16,1,320]{3,1,2,0:T(8,128)(2,1)S(1)}, bf16[4,16,1,320]{3,1,2,0:T(8,128)(2,1)S(1)}, u32[]{:S(2)}, u32[]{:S(2)}) collective-permute-start(bf16[4,16,1,320]{3,1,2,0:T(8,128)(2,1)S(1)} %get-tuple-element.20), channel_id=1, source_target_pairs={{4,0},{8,4},{12,8},{16,12},{20,16},{24,20},{28,24},{0,28},{5,1},{9... | collective-permute-start | bytes 122888 | tf_op jit(solution)/shard_map/ppermute | solution.py:17
  94.0 8.0 %collective-permute-start.10 = (bf16[4,18,320]{2,0,1:T(4,128)(2,1)S(1)}, bf16[4,18,320]{2,0,1:T(4,128)(2,1)S(1)}, u32[]{:S(2)}, u32[]{:S(2)}) collective-permute-start(bf16[4,18,320]{2,0,1:T(4,128)(2,1)S(1)} %bitcast.77), channel_id=1, source_target_pairs={{0,16},{4,20},{8,24},{12,28},{16,0},{20,4},{24,8},{28,12},{1,17},{... | collective-permute-start | bytes 138248 | tf_op jit(solution)/shard_map/ppermute | solution.py:24
  95.6 6.6 %collective-permute-start.11 = (bf16[4,1,18,320]{3,1,2,0:T(2,128)(2,1)S(1)}, bf16[4,1,18,320]{3,1,2,0:T(2,128)(2,1)S(1)}, u32[]{:S(2)}, u32[]{:S(2)}) collective-permute-start(bf16[4,1,18,320]{3,1,2,0:T(2,128)(2,1)S(1)} %get-tuple-element.15), channel_id=1, source_target_pairs={{1,0},{2,1},{3,2},{5,4},{6,5},{7,6},{9,8},{10,9},{11,10},{13,12},{... | collective-permute-start | bytes 138248 | tf_op jit(solution)/shard_map/ppermute | solution.py:17
  96.9 8.8 %collective-permute-start.9 = (bf16[4,1,18,320]{3,1,2,0:T(2,128)(2,1)S(1)}, bf16[4,1,18,320]{3,1,2,0:T(2,128)(2,1)S(1)}, u32[]{:S(2)}, u32[]{:S(2)}) collective-permute-start(bf16[4,1,18,320]{3,1,2,0:T(2,128)(2,1)S(1)} %get-tuple-element.16), channel_id=1, source_target_pairs={{0,1},{1,2},{2,3},{4,5},{5,6},{6,7},{8,9},{9,10},{10,11},{12,13},{... | collective-permute-start | bytes 138248 | tf_op jit(solution)/shard_map/ppermute | solution.py:16
  101.5 4.2 %collective-permute-start.8 = (bf16[4,18,320]{2,0,1:T(4,128)(2,1)S(1)}, bf16[4,18,320]{2,0,1:T(4,128)(2,1)S(1)}, u32[]{:S(2)}, u32[]{:S(2)}) collective-permute-start(bf16[4,18,320]{2,0,1:T(4,128)(2,1)S(1)} %bitcast.76), channel_id=1, source_target_pairs={{0,16},{4,20},{8,24},{12,28},{16,0},{20,4},{24,8},{28,12},{1,17},{... | collective-permute-start | bytes 138248 | tf_op jit(solution)/shard_map/ppermute | solution.py:24
  107.9 1.6 %copy-start.6 = (bf16[3,3,320,320]{3,2,1,0:T(8,128)(2,1)S(1)}, bf16[3,3,320,320]{3,2,1,0:T(8,128)(2,1)}, u32[]{:S(2)}) copy-start(bf16[3,3,320,320]{3,2,1,0:T(8,128)(2,1)} %param.18) | copy-start | bytes 5529604
  107.9 1.6 %copy-start.8 = (f32[320]{0:T(512)S(1)}, f32[320]{0:T(512)}, u32[]{:S(2)}) copy-start(f32[320]{0:T(512)} %param.19) | copy-start | bytes 3844
  115.9 1.1 copy-start.2
